TPU v7x, 128 devices: a whole 4x4x4 slice. The times are simulated.
128 devices in a mesh: walker: 32 (over x, z, core), owner: 4 (over y).
Axes of the slice: x: 4, y: 4, z: 4, core: 2. Of those that a mesh axis runs over, the one named last changes fastest.
Arguments:
- block_input_rows: bfloat16 [2048, 1024, 256], P(('walker', 'owner')), may hold values from -6 to 6
- spin_values: int32 [2048, 1024], P(('walker', 'owner')), may hold values 0 or 1
- conv_weight: bfloat16 [256, 512], replicated, may hold values from -0.25 to 0.25
- conv_bias: float32 [256], replicated, may hold values from -3 to 3
- readout: float32 [256], replicated, may hold values from -0.375 to 0.375
- energies: float32 [2048], P(('walker', 'owner')), may hold values from -1 to 0.1
- basis_out: bfloat16 [256, 256], P(None, 'owner'), may hold values from -0.375 to 0.375
- basis_in: bfloat16 [512, 512], P(None, 'owner'), may hold values from -6 to 6
Outputs:
- moment_stats: float32 [256, 512], P(None, 'owner')
- update: float32 [256, 512], P(None, 'owner')
All inputs are finite; a program needn't handle non-finite values. No bound on the sum of `spin_values` on one device may be relied on, other than what follows from the above.
Results may differ from a plain program's by a relative error of at most 0.025.
Values may be sent and summed in bfloat16 or wider, within the bound.
A program may use at most 128 MiB of HBM per device.

v0:
```python
import jax
import jax.numpy as jnp
from jax import lax
from jax.sharding import PartitionSpec as P

DILATION_STEP = 16


DAMPING = 0.01


def body(
    block_input_rows, spin_values, conv_weight, conv_bias, readout, energies, basis_out, basis_in
):
    local_sample_count = block_input_rows.shape[0]
    chain_site_count = block_input_rows.shape[1]
    channel_count = block_input_rows.shape[2]
    total_samples = local_sample_count * lax.axis_size("walker") * lax.axis_size("owner")
    energy_total = lax.psum(jnp.sum(energies), ("walker", "owner"))
    energy_mean = energy_total / total_samples
    full_out = lax.all_gather(basis_out, "owner", axis=1, tiled=True)
    now_part = jnp.einsum(
        "slc,oc->slo",
        block_input_rows,
        conv_weight[:, channel_count:],
        preferred_element_type=jnp.float32,
    )
    earlier_portion = jnp.einsum(
        "slc,oc->slo",
        block_input_rows,
        conv_weight[:, :channel_count],
        preferred_element_type=jnp.float32,
    )
    delayed_input = jnp.concatenate(
        [
            jnp.zeros((local_sample_count, DILATION_STEP, channel_count), jnp.float32),
            earlier_portion[:, : chain_site_count - DILATION_STEP],
        ],
        axis=1,
    )
    pre_act = now_part + delayed_input + conv_bias
    activation = jnp.tanh(pre_act)
    logit_rows = jnp.sum((block_input_rows.astype(jnp.float32) + activation) * readout, axis=-1)
    target = spin_values.astype(jnp.float32)
    backward_signal = (
        (0.5 * (target - jax.nn.sigmoid(logit_rows)))[:, :, None]
        * readout
        * (1.0 - activation * activation)
    )
    backward_signal = backward_signal.astype(jnp.bfloat16)
    grad_now = jnp.einsum(
        "slo,slc->soc", backward_signal, block_input_rows, preferred_element_type=jnp.float32
    )
    gradient_earlier = jnp.einsum(
        "slo,slc->soc",
        backward_signal[:, DILATION_STEP:],
        block_input_rows[:, : chain_site_count - DILATION_STEP],
        preferred_element_type=jnp.float32,
    )
    gradient = jnp.concatenate([gradient_earlier, grad_now], axis=2).astype(jnp.bfloat16)
    half_proj = jnp.einsum(
        "ok,soc->skc", full_out, gradient, preferred_element_type=jnp.float32
    ).astype(jnp.bfloat16)
    sample_weights = energies - energy_mean
    panel_width = basis_in.shape[1]
    projected = jnp.einsum(
        "skc,cm->skm",
        half_proj,
        lax.all_gather(basis_in, "owner", axis=1, tiled=True),
        preferred_element_type=jnp.float32,
    )
    squares = jnp.sum(projected * projected, axis=0)
    weighted = jnp.einsum("s,skm->km", sample_weights, projected)
    stacked = jnp.stack([squares, weighted], axis=0)
    totals = lax.psum(stacked, ("walker", "owner"))
    owner_panel = lax.dynamic_slice_in_dim(
        totals, lax.axis_index("owner") * panel_width, panel_width, 2
    )
    stats_part = owner_panel[0] / total_samples
    centered = owner_panel[1] / total_samples
    ratio_float = centered / (stats_part + DAMPING)
    scaled_ratio = ratio_float.astype(jnp.bfloat16)
    mixed_basis = jnp.dot(full_out, scaled_ratio, preferred_element_type=jnp.float32).astype(
        jnp.bfloat16
    )
    back_term = jnp.dot(mixed_basis, basis_in.T, preferred_element_type=jnp.float32)
    raw_update = lax.psum_scatter(back_term, "owner", scatter_dimension=1, tiled=True)
    square_total = lax.psum(jnp.sum(raw_update * raw_update), "owner")
    mean_sq = square_total / (channel_count * 2 * channel_count)
    return (stats_part, raw_update / jnp.sqrt(mean_sq + 1e-06))


def solution(mesh):
    in_specs = (
        P(("walker", "owner"), None, None),
        P(("walker", "owner"), None),
        P(),
        P(),
        P(),
        P(("walker", "owner")),
        P(None, "owner"),
        P(None, "owner"),
    )
    out_specs = (P(None, "owner"), P(None, "owner"))
    return jax.shard_map(body, mesh=mesh, in_specs=in_specs, out_specs=out_specs, check_vma=False)
```

profile of v0, /device:TPU:1, one launch (start us, length us, event | category | flops | bytes accessed | tf_op | source)
XLA Modules:
  0.0 354.4 jit_solution(8199990316887416576)
XLA Ops:
  7.2 0.0 copy-start.2
  7.2 0.0 copy-start.6
  7.2 0.0 copy-start.5
  7.2 0.0 all-reduce.3.cloned.1.call-start
  7.2 11.4 %fusion.5 = f32[16,1008,256]{2,1,0:T(8,128)} fusion(bf16[16,1024,256]{2,1,0:T(8,128)(2,1)} %param.8, bf16[256,512]{1,0:T(8,128)(2,1)} %param.10), kind=kOutput, calls=%fused_computation.9 | convolution fusion | flops 2113929216 | bytes 24903680 | tf_op jit(solution)/shard_map/slc,oc->slo/dot_general | solution.py:28
  18.6 0.0 copy-done.2
  18.6 0.0 copy-done.6
  18.6 0.0 copy-done.5
  18.6 0.0 copy-start.3
  18.6 16.8 %multiply_reduce_fusion = (f32[16,1024]{1,0:T(8,128)S(1)}, f32[16,1024,256]{2,1,0:T(8,128)}) fusion(bf16[16,1024,256]{2,1,0:T(8,128)(2,1)} %param.8, f32[256]{0:T(256)S(1)} %copy-done.5, f32[256]{0:T(256)S(1)} %copy-done.6, f32[16,1008,256]{2,1,0:T(8,128)} %fusion.5, bf16[256,512]{1,0:T(8,128)(2,1)S(1)} %copy-done.2), kind=kOutput, calls=%fused_computation.1 | convolution fusion | flops 2172633088 | bytes 50268160 | tf_op jit(solution)/shard_map/slc,oc->slo/dot_general | solution.py:22
  35.5 0.0 copy-done.3
  35.5 10.0 %multiply_convert_fusion = bf16[16,1024,256]{2,1,0:T(8,128)(2,1)} fusion(f32[16,1024,256]{2,1,0:T(8,128)} %get-tuple-element.3, f32[16,1024]{1,0:T(8,128)S(1)} %subtract_multiply_fusion, f32[256]{0:T(256)S(1)} %copy-done.5), kind=kLoop, calls=%fused_computation | loop fusion | flops 20971520 | bytes 25232384 | tf_op jit(solution)/shard_map/convert_element_type | solution.py:50
  45.5 8.2 %convolution_convert_fusion = bf16[16,256,256]{2,1,0:T(8,128)(2,1)S(1)} fusion(bf16[16,1024,256]{2,1,0:T(8,128)(2,1)} %multiply_convert_fusion, bf16[16,1024,256]{2,1,0:T(8,128)(2,1)} %param.8), kind=kOutput, calls=%fused_computation.19 | convolution fusion | flops 2148532224 | bytes 18874368 | tf_op jit(solution)/shard_map/slo,slc->soc/dot_general | solution.py:51
  53.8 0.0 copy-start
  53.8 0.0 copy-start.7
  53.8 0.0 copy-start.4
  53.8 9.6 %fusion.18 = bf16[16,256,256]{2,1,0:T(8,128)(2,1)} fusion(bf16[16,1024,256]{2,1,0:T(8,128)(2,1)} %param.8, bf16[16,1024,256]{2,1,0:T(8,128)(2,1)} %multiply_convert_fusion), kind=kOutput, calls=%fused_computation.18 | convolution fusion | flops 2114977792 | bytes 18612224 | tf_op jit(solution)/shard_map/slo,slc->soc/dot_general | solution.py:54
  63.4 0.0 copy-done
  63.4 13.3 %all_gather.7 = bf16[512,512]{1,0:T(8,128)(2,1)S(1)} all-gather(bf16[512,128]{1,0:T(8,128)(2,1)S(1)} %copy-done), channel_id=1, replica_groups=mesh['walker'=32,'owner'=4] {'owner'}, dimensions={1}, use_global_device_ids=true | all-gather | bytes 655360 | tf_op jit(solution)/shard_map/all_gather | solution.py:69
  76.7 0.0 copy-done.7
  76.7 0.6 reduce_sum.38
  77.3 0.0 copy-done.4
  77.3 9.1 %all_gather.6 = bf16[256,256]{0,1:T(8,128)(2,1)S(1)} all-gather(bf16[256,64]{0,1:T(8,128)(2,1)S(1)} %copy-done.4), channel_id=1, replica_groups=mesh['walker'=32,'owner'=4] {'owner'}, dimensions={1}, use_global_device_ids=true | all-gather | bytes 163840 | tf_op jit(solution)/shard_map/all_gather | solution.py:21
  86.4 71.1 %psum.21 = f32[]{:T(128)} all-reduce(f32[]{:T(128)} %reduce_sum.38), channel_id=1, replica_groups=mesh['walker'=32,'owner'=4] {'walker','owner'}, use_global_device_ids=true, to_apply=%region_3.0 | all-reduce | flops 1 | bytes 8 | tf_op jit(solution)/shard_map/psum | solution.py:19
  158.2 6.2 %multiply_reduce_fusion.1 = (f32[256,512]{1,0:T(8,128)S(1)}, bf16[16,256,512]{2,1,0:T(8,128)(2,1)}) fusion(bf16[512,512]{1,0:T(8,128)(2,1)S(1)} %all_gather.7, bf16[16,256,256]{2,1,0:T(8,128)(2,1)S(1)} %convolution_convert_fusion, bf16[16,256,256]{2,1,0:T(8,128)(2,1)} %fusion.18, bf16[256,256]{0,1:T(8,128)(2,1)S(1)} %all_gather.6), kind=kOutput, calls=%fused_computation.5 | convolution fusion | flops 3237871616 | bytes 9568256 | tf_op jit(solution)/shard_map/skc,cm->skm/dot_general | solution.py:66
  164.4 4.7 %fusion = f32[1,256,512]{2,0,1:T(1,128)S(1)} fusion(bf16[16,256,512]{2,1,0:T(8,128)(2,1)} %get-tuple-element.5, f32[16]{0:T(128)S(1)} %copy-done.7, f32[]{:T(128)S(6)} %div.29), kind=kOutput, calls=%fused_computation.3 | convolution fusion | flops 4194320 | bytes 4718660 | tf_op jit(solution)/shard_map/s,skm->km/dot_general | solution.py:73
  169.1 1.1 pad_maximum_fusion
  170.2 0.0 all-reduce.3.cloned.1.call-update
  170.3 0.0 reduce-scatter.2.cloned.1.call-start
  170.3 144.6 %all-reduce.3.cloned.1.call-done = f32[2,256,512]{2,1,0:T(8,128)} async-done(((f32[2,256,512]{2,1,0:T(8,128)}), f32[2,256,512]{2,1,0:T(8,128)}) %all-reduce.3.cloned.1.call-update) | async-done | bytes 1048592 | tf_op jit(solution)/shard_map/psum | solution.py:75
  314.9 0.9 fusion.28
  315.8 0.0 copy-start.1
  315.9 2.2 fusion.23
  318.1 0.0 reduce-scatter.2.cloned.1.call-update
  318.1 18.5 %reduce-scatter.2.cloned.1.call-done = f32[256,128]{1,0:T(8,128)} async-done(((f32[256,512]{1,0:T(8,128)}), f32[256,128]{1,0:T(8,128)}) %reduce-scatter.2.cloned.1.call-update) | async-done | bytes 131088 | tf_op jit(solution)/shard_map/reduce_scatter | solution.py:87
  336.6 1.5 multiply_reduce_fusion.2
  338.1 7.1 %psum.23 = f32[]{:T(128)} all-reduce(f32[]{:T(128)} %multiply_reduce_fusion.2), channel_id=1, replica_groups=mesh['walker'=32,'owner'=4] {'owner'}, use_global_device_ids=true, to_apply=%region_7.0 | all-reduce | flops 1 | bytes 8 | tf_op jit(solution)/shard_map/psum | solution.py:88
  346.0 1.6 broadcast_divide_fusion
  347.5 0.0 copy-done.1
  (2 shorter events, 0.1 us)
Async XLA Ops:
  7.2 11.5 %copy-start.2 = (bf16[256,512]{1,0:T(8,128)(2,1)S(1)}, bf16[256,512]{1,0:T(8,128)(2,1)}, u32[]{:S(2)}) copy-start(bf16[256,512]{1,0:T(8,128)(2,1)} %param.10) | copy-start | bytes 786436
  7.2 11.5 %copy-start.6 = (f32[256]{0:T(256)S(1)}, f32[256]{0:T(256)}, u32[]{:S(2)}) copy-start(f32[256]{0:T(256)} %param.11) | copy-start | bytes 3076
  7.2 11.4 %copy-start.5 = (f32[256]{0:T(256)S(1)}, f32[256]{0:T(256)}, u32[]{:S(2)}) copy-start(f32[256]{0:T(256)} %param.12) | copy-start | bytes 3076
  7.2 307.7 %all-reduce.3.cloned.1.call-start = ((), (), s32[]{:S(2)}) async-start(), calls=%async_computation.1 | async-start | bytes 2097152 | tf_op jit(solution)/shard_map/psum | solution.py:75
  18.6 16.8 %copy-start.3 = (s32[16,1024]{1,0:T(8,128)S(1)}, s32[16,1024]{1,0:T(8,128)}, u32[]{:S(2)}) copy-start(s32[16,1024]{1,0:T(8,128)} %param.9) | copy-start | bytes 196612
  53.8 9.6 %copy-start = (bf16[512,128]{1,0:T(8,128)(2,1)S(1)}, bf16[512,128]{1,0:T(8,128)(2,1)}, u32[]{:S(2)}) copy-start(bf16[512,128]{1,0:T(8,128)(2,1)} %param.15) | copy-start | bytes 393220
  53.8 22.9 %copy-start.7 = (f32[16]{0:T(128)S(1)}, f32[16]{0:T(128)}, u32[]{:S(2)}) copy-start(f32[16]{0:T(128)} %param.13) | copy-start | bytes 196
  53.8 23.5 %copy-start.4 = (bf16[256,64]{0,1:T(8,128)(2,1)S(1)}, bf16[256,64]{0,1:T(8,128)(2,1)}, u32[]{:S(2)}) copy-start(bf16[256,64]{0,1:T(8,128)(2,1)} %param.14) | copy-start | bytes 98308
  170.3 166.3 %reduce-scatter.2.cloned.1.call-start = ((), (), s32[]{:S(2)}) async-start(), calls=%async_computation.2 | async-start | bytes 655360 | tf_op jit(solution)/shard_map/reduce_scatter | solution.py:87
  315.8 31.7 %copy-start.1 = (f32[256,128]{1,0:T(8,128)}, f32[256,128]{1,0:T(8,128)S(1)}, u32[]{:S(2)}) copy-start(f32[256,128]{1,0:T(8,128)S(1)} %fusion.28) | copy-start | bytes 393220
Sparse Core Ops, SparseCore 0:
  170.4 144.4 all-reduce.2
  318.2 18.3 reduce-scatter.1
where the time goes:
time: 358 us; the launch traced here: 354 us
  waiting for transfers between devices  163 us (46%)
  blocking collectives  101 us (28%)
  matrix products  59.2 us (17%)
  other arithmetic  15.8 us (4%)
  between operations  15.5 us (4%)
    psum x1, waiting for transfers between devices, body(): totals = lax.psum(stacked, ('walker', 'owner'))  145 us
    psum x1, blocking collectives, body(): energy_total = lax.psum(jnp.sum(energies), ('walker', 'owner'))  71.1 us
    reduce_scatter x1, waiting for transfers between devices, body(): lax.psum_scatter(back_term, 'owner', scatter_dimension=1, tiled=True)  18.5 us
    dot_general x1, matrix products, body(): jnp.einsum('slc,oc->slo', block_input_rows, conv_weight[:, channel_count:...  16.8 us
    all_gather x1, blocking collectives, body(): lax.all_gather(basis_in, 'owner', axis=1, tiled=True)  13.3 us
    dot_general x1, matrix products, body(): jnp.einsum('slc,oc->slo', block_input_rows, conv_weight[:, :channel_count...  11.4 us
    convert_element_type x1, other arithmetic, body(): backward_signal = backward_signal.astype(jnp.bfloat16)  10 us
    dot_general x1, matrix products, body(): jnp.einsum('slo,slc->soc', backward_signal[:, DILATION_STEP:], block_inpu...  9.59 us
  transfers between devices with their start and end apart: 2, of which 2 were waited for; matrix products, arithmetic and copies ran while one was open for 0% of the time, Pallas kernels for 0%

commit v1 on v0

v1 whole, which is shorter than its diff:
```python
import jax
import jax.numpy as jnp
from jax import lax
from jax.experimental import pallas as pl
from jax.experimental.pallas import tpu as pltpu
from jax.sharding import PartitionSpec as P

DILATION_STEP = 16
DAMPING = 0.01
BF = jnp.bfloat16
F32 = jnp.float32
MESH = pl.DeviceIdType.MESH

GROUPS = 16
OWNERS = 4
LANES = 128


def dot_nt(a, b):
    return lax.dot_general(a, b, (((1,), (1,)), ((), ())), preferred_element_type=F32)


def dot_nn(a, b):
    return jnp.dot(a, b, preferred_element_type=F32)


def wide(value, count):
    return jnp.concatenate([value] * count, axis=1) if count > 1 else value


def kernel(
    x_hbm, spin_ref, w_ref, bias_ref, readout_ref, e_ref, bo_ref, bi_ref,
    stats_ref, update_ref,
    xbuf, back, grads, halves, bo_full, bi_full, bias_col, read_col, read_rows,
    e_out, e_in, core_out, core_in, own, y_out, y_in, plane_out, plane_in, plane_own,
    ring, ratio_full, stats_out, stats_in, raw_buf,
    x_sem, basis_send, basis_recv, e_send, e_recv, core_send, core_recv,
    y_send, y_recv, plane_send, plane_recv, ring_send, ring_recv, last_send, last_recv,
):
    samples, sites, channels = x_hbm.shape
    pad = DILATION_STEP
    total_samples = samples * 128
    walker = lax.axis_index("walker")
    owner = lax.axis_index("owner")
    core = lax.rem(walker, 2)
    group = walker // 2
    gx, gz = group // 4, lax.rem(group, 4)
    twin = (group * 2 + (1 - core), owner)

    def across(step):
        return (walker, lax.rem(owner + step, OWNERS))

    def plane(dx, dz):
        return lax.rem(gx + dx, 4) * 4 + lax.rem(gz + dz, 4)

    def plane_id(dx, dz):
        return (plane(dx, dz) * 2 + core, owner)

    plane_steps = [(k // 4, k % 4) for k in range(1, GROUPS)]
    peers = [twin] + [across(d) for d in (1, 2, 3)] + [plane_id(*s) for s in plane_steps]

    barrier = pltpu.get_barrier_semaphore()
    for peer in peers:
        pl.semaphore_signal(barrier, inc=1, device_id=peer, device_id_type=MESH)

    def load(i):
        return pltpu.make_async_copy(x_hbm.at[i], xbuf.at[i, pl.ds(pad, sites), :], x_sem.at[i])

    for i in range(samples):
        load(i).start()

    def send(src, dst, ssem, rsem, peer):
        return pltpu.make_async_remote_copy(
            src_ref=src, dst_ref=dst, send_sem=ssem, recv_sem=rsem,
            device_id=peer, device_id_type=MESH,
        )

    bias_col[...] = jnp.broadcast_to(bias_ref[...], (LANES, channels)).T
    read_col[...] = jnp.broadcast_to(readout_ref[...], (LANES, channels)).T
    r = readout_ref[...]
    hi = r.astype(BF).astype(F32)
    mid = (r - hi).astype(BF).astype(F32)
    low = r - hi - mid
    row = lax.broadcasted_iota(jnp.int32, (16, channels), 0)
    spread = jnp.where(row == 0, hi, jnp.where(row == 1, mid, jnp.where(row == 2, low, 0.0)))
    read_rows[...] = spread.astype(BF)
    for i in range(samples):
        xbuf[i, 0:pad, :] = jnp.zeros((pad, channels), BF)

    own_rows = pl.ds(pl.multiple_of(owner * 64, 64), 64)
    own_cols = pl.ds(pl.multiple_of(owner * LANES, LANES), LANES)
    bo_full[own_rows, :] = bo_ref[...]
    bi_full[:, own_cols] = bi_ref[...]

    def basis_copies():
        out = []
        for d in (1, 2, 3):
            out.append(send(bo_ref, bo_full.at[own_rows, :], basis_send.at[d - 1],
                            basis_recv.at[d - 1], across(d)))
            out.append(send(bi_ref, bi_full.at[:, own_cols], basis_send.at[d + 2],
                            basis_recv.at[d + 2], across(d)))
        return out

    e_sum = e_ref[0]
    for i in range(1, samples):
        e_sum = e_sum + e_ref[i]
    e_out[0] = jnp.full((8, LANES), e_sum, F32)
    stages = [
        [twin],
        [across(d) for d in (1, 2, 3)],
        [plane_id(d, 0) for d in (1, 2, 3)],
        [plane_id(0, d) for d in (1, 2, 3)],
    ]
    first_slot = [0, 1, 4, 7]

    def energy_copies(stage):
        base = first_slot[stage]
        return [send(e_out.at[stage], e_in.at[base + k], e_send.at[base + k],
                     e_recv.at[base + k], peer) for k, peer in enumerate(stages[stage])]

    def energy_finish(stage):
        copies = energy_copies(stage)
        for c in copies:
            c.wait()
        total = e_out[stage]
        for k in range(len(copies)):
            total = total + e_in[first_slot[stage] + k]
        e_out[stage + 1] = total

    chunk = 256

    @pl.loop(0, samples)
    def _(i):
        @pl.when(i == 1)
        def _():
            pl.semaphore_wait(barrier, len(peers))
            for c in energy_copies(0):
                c.start()
            for c in basis_copies():
                c.start()

        for stage in range(4):
            @pl.when(i == 4 + 3 * stage)
            def _(stage=stage):
                energy_finish(stage)
                if stage < 3:
                    for c in energy_copies(stage + 1):
                        c.start()

        load(i).wait()
        for c in range(sites // chunk):
            lo = c * chunk
            x_prev = xbuf[i, lo:lo + chunk, :]
            x_now = xbuf[i, lo + pad:lo + pad + chunk, :]
            pre = dot_nt(w_ref[:, :channels], x_prev) + dot_nt(w_ref[:, channels:], x_now)
            x_logit = dot_nt(read_rows[...], x_now)
            act = jnp.tanh(pre + wide(bias_col[...], chunk // LANES))
            logit = jnp.sum(act * wide(read_col[...], chunk // LANES), axis=0, keepdims=True)
            logit = logit + jnp.sum(x_logit, axis=0, keepdims=True)
            target = spin_ref[pl.ds(i, 1), lo:lo + chunk].astype(F32)
            signal = 0.5 * (target - jax.nn.sigmoid(logit))
            back[:, lo:lo + chunk] = (signal * (1.0 - act * act)).astype(BF)
        scale = wide(read_col[...], channels // LANES)
        b = back[...]
        grads[i, :, :channels] = (dot_nn(b, xbuf[i, :sites, :]) * scale).astype(BF)
        grads[i, :, channels:] = (dot_nn(b, xbuf[i, pad:, :]) * scale).astype(BF)

    for c in basis_copies():
        c.wait()

    @pl.loop(0, samples)
    def _(i):
        halves[i] = dot_nn(bo_full[...], grads[i]).astype(BF)

    e_mean = jnp.broadcast_to(e_out[4][0:1, :], (64, LANES)) * (1.0 / total_samples)

    def project(first, tile):
        q, m = tile // 2, tile % 2
        rows = pl.ds(pl.multiple_of(first + q * 64, 64), 64)
        lhs = halves[:, rows, :].reshape(samples * 64, 2 * channels)
        p = dot_nn(lhs, bi_full[:, m * 256:(m + 1) * 256])
        squares = jnp.zeros((64, 256), F32)
        weighted = jnp.zeros((64, 256), F32)
        for n in range(samples):
            pn = p[n * 64:(n + 1) * 64]
            squares = squares + pn * pn
            weighted = weighted + pn * wide(e_ref[n] - e_mean, 2)
        out = []
        for k in range(2):
            cols = slice(k * LANES, (k + 1) * LANES)
            out.append((2 * m + k, q * 8, jnp.concatenate(
                [squares[:, cols].reshape(8, 8, LANES), weighted[:, cols].reshape(8, 8, LANES)],
                axis=1)))
        return out

    for tile in range(4):
        for o, g, block in project((1 - core) * 128, tile):
            core_out[o, g:g + 8] = block.astype(BF)
    core_copy = send(core_out, core_in, core_send, core_recv, twin)
    core_copy.start()
    for tile in range(4):
        for o, g, block in project(core * 128, tile):
            own[o, g:g + 8] = block
    core_copy.wait()

    y_copies = []
    for d in (1, 2, 3):
        o = lax.rem(owner + d, OWNERS)
        y_out[d - 1] = (own[o] + core_in[o].astype(F32)).astype(BF)
        y_copies.append(send(y_out.at[d - 1], y_in.at[d - 1], y_send.at[d - 1],
                             y_recv.at[d - 1], across(d)))
        y_copies[-1].start()
    total = own[owner] + core_in[owner].astype(F32)
    for d in (1, 2, 3):
        y_copies[d - 1].wait()
        total = total + y_in[d - 1].astype(F32)

    plane_own[...] = total
    plane_out[...] = total.astype(BF)
    plane_copies = []
    for k, step in enumerate(plane_steps):
        plane_copies.append(send(plane_out.at[plane(*step)], plane_in.at[k], plane_send.at[k],
                                 plane_recv.at[k], plane_id(*step)))
        plane_copies[-1].start()
    final = plane_own[group]
    for k in range(GROUPS - 1):
        plane_copies[k].wait()
        final = final + plane_in[k].astype(F32)

    final = final * (1.0 / total_samples)
    moments = final[0:8]
    ratio = final[8:16] / (moments + DAMPING)
    ring[group] = jnp.concatenate([ratio, moments], axis=0).astype(BF)
    ring_copies = []
    for k, step in enumerate(plane_steps):
        ring_copies.append(send(ring.at[group], ring.at[group], ring_send.at[k],
                                ring_recv.at[k], plane_id(*step)))
        ring_copies[-1].start()
    for c in ring_copies:
        c.wait()

    both = ring[...].astype(F32)
    my_rows = pl.ds(pl.multiple_of(core * 128, 128), 128)
    ratio_full[owner, my_rows, :] = both[:, 0:8, :].reshape(128, LANES).astype(BF)
    moments = both[:, 8:16, :].reshape(128, LANES)
    stats_out[...] = moments.astype(BF)
    last = [send(ratio_full.at[owner, my_rows, :], ratio_full.at[owner, my_rows, :],
                 last_send.at[d - 1], last_recv.at[d - 1], across(d)) for d in (1, 2, 3)]
    for c in last:
        c.start()
    to_twin = [send(ratio_full.at[owner, my_rows, :], ratio_full.at[owner, my_rows, :],
                    last_send.at[3], last_recv.at[3], twin),
               send(stats_out, stats_in, last_send.at[4], last_recv.at[4], twin)]
    for c in to_twin:
        c.start()
    stats_ref[my_rows, :] = stats_out[...].astype(F32)
    for d in (1, 2, 3):
        last[d - 1].wait()
        o = lax.rem(owner + OWNERS - d, OWNERS)
        to_twin.append(send(ratio_full.at[o, my_rows, :], ratio_full.at[o, my_rows, :],
                            last_send.at[4 + d], last_recv.at[4 + d], twin))
        to_twin[-1].start()
    for c in to_twin:
        c.wait()
    twin_rows = pl.ds(pl.multiple_of((1 - core) * 128, 128), 128)
    stats_ref[twin_rows, :] = stats_in[...].astype(F32)

    ratio_all = jnp.concatenate([ratio_full[o] for o in range(OWNERS)], axis=1)
    mixed = lax.dot_general(bo_full[...], ratio_all, (((0,), (0,)), ((), ())),
                            preferred_element_type=F32).astype(BF)
    raw = dot_nt(mixed, bi_full[...])
    for o in range(OWNERS):
        raw_buf[o] = raw[:, o * LANES:(o + 1) * LANES]
    squares = jnp.sum(jnp.sum(raw * raw, axis=0, keepdims=True), axis=1, keepdims=True)
    mean_sq = squares * (1.0 / (channels * 2 * channels))
    update_ref[...] = raw_buf[owner] / jnp.sqrt(mean_sq + 1e-06)


def body(
    block_input_rows, spin_values, conv_weight, conv_bias, readout, energies, basis_out, basis_in
):
    samples, sites, channels = block_input_rows.shape
    vmem = pl.BlockSpec(memory_space=pltpu.VMEM)
    dma = pltpu.SemaphoreType.DMA
    return pl.pallas_call(
        kernel,
        out_shape=(
            jax.ShapeDtypeStruct((channels, LANES), F32),
            jax.ShapeDtypeStruct((channels, LANES), F32),
        ),
        in_specs=[pl.BlockSpec(memory_space=pl.ANY), vmem, vmem, vmem, vmem,
                  pl.BlockSpec(memory_space=pltpu.SMEM), vmem, vmem],
        out_specs=(vmem, vmem),
        scratch_shapes=[
            pltpu.VMEM((samples, sites + DILATION_STEP, channels), BF),
            pltpu.VMEM((channels, sites), BF),
            pltpu.VMEM((samples, channels, 2 * channels), BF),
            pltpu.VMEM((samples, channels, 2 * channels), BF),
            pltpu.VMEM((channels, channels), BF),
            pltpu.VMEM((2 * channels, 2 * channels), BF),
            pltpu.VMEM((channels, LANES), F32),
            pltpu.VMEM((channels, LANES), F32),
            pltpu.VMEM((16, channels), BF),
            pltpu.VMEM((5, 8, LANES), F32),
            pltpu.VMEM((10, 8, LANES), F32),
            pltpu.VMEM((OWNERS, GROUPS, 16, LANES), BF),
            pltpu.VMEM((OWNERS, GROUPS, 16, LANES), BF),
            pltpu.VMEM((OWNERS, GROUPS, 16, LANES), F32),
            pltpu.VMEM((3, GROUPS, 16, LANES), BF),
            pltpu.VMEM((3, GROUPS, 16, LANES), BF),
            pltpu.VMEM((GROUPS, 16, LANES), BF),
            pltpu.VMEM((GROUPS - 1, 16, LANES), BF),
            pltpu.VMEM((GROUPS, 16, LANES), F32),
            pltpu.VMEM((GROUPS, 16, LANES), BF),
            pltpu.VMEM((OWNERS, channels, LANES), BF),
            pltpu.VMEM((channels // 2, LANES), BF),
            pltpu.VMEM((channels // 2, LANES), BF),
            pltpu.VMEM((OWNERS, channels, LANES), F32),
            dma((samples,)),
            dma((6,)), dma((6,)),
            dma((10,)), dma((10,)),
            dma(()), dma(()),
            dma((3,)), dma((3,)),
            dma((GROUPS - 1,)), dma((GROUPS - 1,)),
            dma((GROUPS - 1,)), dma((GROUPS - 1,)),
            dma((8,)), dma((8,)),
        ],
        compiler_params=pltpu.CompilerParams(
            collective_id=0, has_side_effects=True, vmem_limit_bytes=56 << 20),
    )(
        block_input_rows, spin_values, conv_weight,
        conv_bias.reshape(1, channels), readout.reshape(1, channels), energies,
        basis_out.T, basis_in,
    )


def solution(mesh):
    in_specs = (
        P(("walker", "owner"), None, None),
        P(("walker", "owner"), None),
        P(),
        P(),
        P(),
        P(("walker", "owner")),
        P(None, "owner"),
        P(None, "owner"),
    )
    out_specs = (P(None, "owner"), P(None, "owner"))
    return jax.shard_map(body, mesh=mesh, in_specs=in_specs, out_specs=out_specs, check_vma=False)
```

time: 358 us -> 61.8 us (0.17)
  waiting for transfers between devices: 163 us -> 0 us
  blocking collectives: 101 us -> 0 us
  matrix products: 59.2 us -> 0 us
  Pallas kernels: 0 us -> 57.9 us
  other arithmetic: 15.8 us -> 0 us
  between operations: 15.5 us -> 0.64 us
    psum x1 -> x0, waiting for transfers between devices: 145 us -> none  [body(): totals = lax.psum(stacked, ('walker', 'owner'))]
    psum x2 -> x0, blocking collectives: 78.3 us -> none  [the longest x1 71.1 us: body(): energy_total = lax.psum(jnp.sum(energies), ('walker', 'owner'))]
    dot_general x7 -> x0, matrix products: 59.2 us -> none  [the longest x1 16.8 us: body(): jnp.einsum('slc,oc->slo', block_input_rows, conv_weight[:, channel_count:...]
    pallas_call x0 -> x1, Pallas kernels: none -> 57.9 us  [body(): pl.pallas_call(kernel, out_shape=(jax.ShapeDtypeStruct((channels, LANES),...]
    all_gather x2 -> x0, blocking collectives: 22.4 us -> none  [the longest x1 13.3 us: body(): lax.all_gather(basis_in, 'owner', axis=1, tiled=True)]
    reduce_scatter x1 -> x0, waiting for transfers between devices: 18.5 us -> none  [body(): lax.psum_scatter(back_term, 'owner', scatter_dimension=1, tiled=True)]
    convert_element_type x1 -> x0, other arithmetic: 10 us -> none  [body(): backward_signal = backward_signal.astype(jnp.bfloat16)]
  transfers between devices with their start and end apart: 2 -> 0, of which waited for: 2 -> 0; matrix products, arithmetic and copies ran while one was open for 0% -> 0% of each run, Pallas kernels for 0% -> 0%
where the time goes in v1:
time: 61.8 us; the launch traced here: 61.6 us
  Pallas kernels  57.9 us (94%)
  local copies, waits for them, and re-layouts  3.14 us (5%)
  between operations  0.64 us (1%)
    pallas_call x1, Pallas kernels, body(): pl.pallas_call(kernel, out_shape=(jax.ShapeDtypeStruct((channels, LANES),...  57.9 us
    unnamed x2, local copies, waits for them, and re-layouts  3.14 us

profile of v1, /device:TPU:1, one launch (start us, length us, event | category | flops | bytes accessed | tf_op | source)
XLA Modules:
  0.0 61.6 jit_solution(6829526111429265901)
XLA Ops:
  0.6 57.9 %shard_map.95 = (f32[256,128]{1,0:T(8,128)}, f32[256,128]{1,0:T(8,128)}) custom-call(bf16[16,1024,256]{2,1,0:T(8,128)(2,1)} %x_hbm.1, s32[16,1024]{1,0:T(8,128)} %spin_ref.1, bf16[256,512]{1,0:T(8,128)(2,1)} %w_ref.1, f32[1,256]{1,0:T(1,128)} %bitcast.4, f32[1,256]{1,0:T(1,128)} %bitcast.5, f32[16]{0:T(128)} %e_ref.1, bf16[64,256]{1,0:T(8,128)(2,1)} %bitcast.3, ...), custom_call_target="tpu_custom_call" | custom-call | tf_op jit(solution)/shard_map/pallas_call | solution.py:285
  58.5 1.6 %copy.12 = f32[256,128]{1,0:T(8,128)} copy(f32[256,128]{1,0:T(8,128)} %get-tuple-element.4) | data formatting | bytes 262144
  60.1 1.6 %copy.13 = f32[256,128]{1,0:T(8,128)} copy(f32[256,128]{1,0:T(8,128)} %get-tuple-element.5) | data formatting | bytes 262144

commit v2 on v1

v2 whole, which is shorter than its diff:
```python
import jax
import jax.numpy as jnp
from jax import lax
from jax.experimental import pallas as pl
from jax.experimental.pallas import tpu as pltpu
from jax.sharding import PartitionSpec as P

DILATION_STEP = 16
DAMPING = 0.01
BF = jnp.bfloat16
F32 = jnp.float32
MESH = pl.DeviceIdType.MESH

GROUPS = 16
OWNERS = 4
LANES = 128


def dot_nt(a, b):
    return lax.dot_general(a, b, (((1,), (1,)), ((), ())), preferred_element_type=F32)


def dot_nn(a, b):
    return jnp.dot(a, b, preferred_element_type=F32)


def wide(value, count):
    return jnp.concatenate([value] * count, axis=1) if count > 1 else value


OFFSETS = sorted(
    [(dx, dy, dz) for dx in range(4) for dy in range(4) for dz in range(4)][1:],
    key=lambda step: -sum(min(d, 4 - d) for d in step),
)


def kernel(
    x_hbm, spin_ref, w_ref, bias_ref, readout_ref, e_ref, bo_ref, bi_ref,
    stats_ref, update_ref,
    xbuf, back_a, back_b, grads, halves, bo_full, bi_full, bias_col, read_col, weight,
    e_out, e_in, core_out, core_in, own, sum_out, sum_in, ring, ring_twin, raw_buf,
    x_sem, basis_send, basis_recv, e_send, e_recv, core_send, core_recv,
    sum_send, sum_recv, ring_send, ring_recv, last_send, last_recv,
):
    samples, sites, channels = x_hbm.shape
    pad = DILATION_STEP
    total_samples = samples * 128
    walker = lax.axis_index("walker")
    owner = lax.axis_index("owner")
    core = lax.rem(walker, 2)
    group = walker // 2
    gx, gz = group // 4, lax.rem(group, 4)
    xs = [gx * 4] + [lax.rem(gx + d, 4) * 4 for d in (1, 2, 3)]
    zs = [gz] + [lax.rem(gz + d, 4) for d in (1, 2, 3)]
    ys = [owner] + [lax.rem(owner + d, 4) for d in (1, 2, 3)]

    def chip(dx, dy, dz):
        return ((xs[dx] + zs[dz]) * 2 + core, ys[dy])

    twin = (group * 2 + (1 - core), owner)
    peers = [twin] + [chip(*s) for s in OFFSETS]

    barrier = pltpu.get_barrier_semaphore()
    for peer in peers:
        pl.semaphore_signal(barrier, inc=1, device_id=peer, device_id_type=MESH)

    def load(i):
        return pltpu.make_async_copy(x_hbm.at[i], xbuf.at[i, pl.ds(pad, sites), :], x_sem.at[i])

    for i in range(samples):
        load(i).start()

    def send(src, dst, ssem, rsem, peer):
        return pltpu.make_async_remote_copy(
            src_ref=src, dst_ref=dst, send_sem=ssem, recv_sem=rsem,
            device_id=peer, device_id_type=MESH,
        )

    bias_col[...] = jnp.broadcast_to(bias_ref[...], (LANES, channels)).T
    read_col[...] = jnp.broadcast_to(readout_ref[...], (LANES, channels)).T
    r = readout_ref[...]
    hi = r.astype(BF).astype(F32)
    mid = (r - hi).astype(BF).astype(F32)
    low = r - hi - mid
    row = lax.broadcasted_iota(jnp.int32, (16, channels), 0)
    spread = jnp.where(row == 0, hi, jnp.where(row == 1, mid, jnp.where(row == 2, low, 0.0)))
    weight[:channels, :] = w_ref[...]
    weight[channels:, :channels] = jnp.zeros((16, channels), BF)
    weight[channels:, channels:] = spread.astype(BF)
    for i in range(samples):
        xbuf[i, 0:pad, :] = jnp.zeros((pad, channels), BF)

    own_rows = pl.ds(pl.multiple_of(owner * 64, 64), 64)
    own_cols = pl.ds(pl.multiple_of(owner * LANES, LANES), LANES)
    bi_half = pl.ds(pl.multiple_of(core * channels, channels), channels)
    bo_full[own_rows, :] = bo_ref[...]
    bi_full[:, own_cols] = bi_ref[...]

    def bo_copies():
        return [send(bo_ref, bo_full.at[own_rows, :], basis_send.at[d - 1],
                     basis_recv.at[d - 1], chip(0, d, 0)) for d in (1, 2, 3)]

    def bi_copies():
        return [send(bi_ref.at[bi_half, :], bi_full.at[bi_half, own_cols], basis_send.at[d + 2],
                     basis_recv.at[d + 2], chip(0, d, 0)) for d in (1, 2, 3)]

    def bi_relays():
        out = []
        for d in (1, 2, 3):
            cols = pl.ds(pl.multiple_of(ys[d] * LANES, LANES), LANES)
            part = bi_full.at[bi_half, cols]
            out.append(send(part, part, basis_send.at[d + 5], basis_recv.at[d + 5], twin))
        return out

    e_sum = e_ref[0]
    for i in range(1, samples):
        e_sum = e_sum + e_ref[i]
    e_out[0] = jnp.full((8, LANES), e_sum, F32)
    stages = [
        [twin],
        [chip(0, d, 0) for d in (1, 2, 3)],
        [chip(k // 4, 0, k % 4) for k in range(1, GROUPS)],
    ]
    first_slot = [0, 1, 4]

    def energy_copies(stage):
        base = first_slot[stage]
        return [send(e_out.at[stage], e_in.at[base + k], e_send.at[base + k],
                     e_recv.at[base + k], peer) for k, peer in enumerate(stages[stage])]

    def energy_start(stage):
        for c in energy_copies(stage):
            c.start()

    def energy_finish(stage):
        copies = energy_copies(stage)
        for c in copies:
            c.wait()
        total = e_out[stage]
        for k in range(len(copies)):
            total = total + e_in[first_slot[stage] + k]
        e_out[stage + 1] = total

    chunk = 256

    def forward(i, back):
        for c in range(sites // chunk):
            lo = c * chunk
            x_prev = xbuf[i, lo:lo + chunk, :]
            x_now = xbuf[i, lo + pad:lo + pad + chunk, :]
            out = dot_nt(weight[...], jnp.concatenate([x_prev, x_now], axis=1))
            act = jnp.tanh(out[:channels] + wide(bias_col[...], chunk // LANES))
            logit = jnp.sum(act * wide(read_col[...], chunk // LANES), axis=0, keepdims=True)
            logit = logit + jnp.sum(out[channels:], axis=0, keepdims=True)
            target = spin_ref[pl.ds(i, 1), lo:lo + chunk].astype(F32)
            signal = 0.5 * (target - jax.nn.sigmoid(logit))
            back[:, lo:lo + chunk] = (signal * (1.0 - act * act)).astype(BF)

    def gradient(i, back):
        scale = wide(read_col[...], channels // LANES)
        b = back[...]
        grads[i, :, :channels] = (dot_nn(b, xbuf[i, :sites, :]) * scale).astype(BF)
        grads[i, :, channels:] = (dot_nn(b, xbuf[i, pad:, :]) * scale).astype(BF)

    @pl.loop(0, samples // 2)
    def _(j):
        @pl.when(j == 1)
        def _():
            pl.semaphore_wait(barrier, len(peers))
            energy_start(0)

        @pl.when(j == 2)
        def _():
            energy_finish(0)
            energy_start(1)
            for c in bo_copies() + bi_copies():
                c.start()

        @pl.when(j == 5)
        def _():
            energy_finish(1)
            energy_start(2)

        @pl.when(j == 7)
        def _():
            for c in bi_copies():
                c.wait()
            for c in bi_relays():
                c.start()

        load(2 * j).wait()
        load(2 * j + 1).wait()
        forward(2 * j, back_a)
        forward(2 * j + 1, back_b)
        gradient(2 * j, back_a)
        gradient(2 * j + 1, back_b)

    for c in bo_copies():
        c.wait()

    @pl.loop(0, samples // 8)
    def _(j):
        for u in range(8):
            halves[8 * j + u] = dot_nn(bo_full[...], grads[8 * j + u]).astype(BF)

    energy_finish(2)
    for c in bi_relays():
        c.wait()

    e_mean = jnp.broadcast_to(e_out[3][0:1, :], (64, LANES)) * (1.0 / total_samples)

    def project(first, tile):
        q, m = tile // 2, tile % 2
        rows = pl.ds(pl.multiple_of(first + q * 64, 64), 64)
        lhs = halves[:, rows, :].reshape(samples * 64, 2 * channels)
        p = dot_nn(lhs, bi_full[:, m * 256:(m + 1) * 256])
        squares = jnp.zeros((64, 256), F32)
        weighted = jnp.zeros((64, 256), F32)
        for n in range(samples):
            pn = p[n * 64:(n + 1) * 64]
            squares = squares + pn * pn
            weighted = weighted + pn * wide(e_ref[n] - e_mean, 2)
        out = []
        for k in range(2):
            cols = slice(k * LANES, (k + 1) * LANES)
            out.append((2 * m + k, q * 8, jnp.concatenate(
                [squares[:, cols].reshape(8, 8, LANES), weighted[:, cols].reshape(8, 8, LANES)],
                axis=1)))
        return out

    for tile in range(4):
        for o, g, block in project((1 - core) * 128, tile):
            core_out[o, g:g + 8] = block.astype(BF)
    core_copy = send(core_out, core_in, core_send, core_recv, twin)
    core_copy.start()
    for tile in range(4):
        for o, g, block in project(core * 128, tile):
            own[o, g:g + 8] = block
    core_copy.wait()

    sum_out[...] = (own[...] + core_in[...].astype(F32)).astype(BF)
    sum_copies = []
    for k, (dx, dy, dz) in enumerate(OFFSETS):
        sum_copies.append(send(sum_out.at[ys[dy], xs[dx] + zs[dz]], sum_in.at[k], sum_send.at[k],
                               sum_recv.at[k], chip(dx, dy, dz)))
        sum_copies[-1].start()
    final = sum_out[owner, group].astype(F32)
    for c in sum_copies:
        c.wait_recv()
    for k in range(len(OFFSETS)):
        final = final + sum_in[k].astype(F32)

    final = final * (1.0 / total_samples)
    moments = final[0:8]
    ratio = final[8:16] / (moments + DAMPING)
    ring[owner, group] = jnp.concatenate([ratio, moments], axis=0).astype(BF)
    tile = ring.at[owner, group]
    ring_copies = {}
    for k, step in enumerate(OFFSETS):
        ring_copies[step] = send(tile, tile, ring_send.at[k], ring_recv.at[k], chip(*step))
        ring_copies[step].start()

    to_twin = []
    for d in (0, 1, 3, 2):
        for step in OFFSETS:
            if step[1] == (4 - d) % 4:
                ring_copies[step].wait_recv()
        to_twin.append(send(ring.at[ys[d]], ring_twin.at[ys[d]], last_send.at[d],
                            last_recv.at[d], twin))
        to_twin[-1].start()

    def back_project(tiles, half):
        both = tiles[...].astype(F32)
        rows = pl.ds(pl.multiple_of(half * 128, 128), 128)
        ratios = jnp.concatenate(
            [both[o, :, 0:8, :].reshape(128, LANES).astype(BF) for o in range(OWNERS)], axis=1)
        stats_ref[rows, :] = tiles[owner].astype(F32)[:, 8:16, :].reshape(128, LANES)
        return lax.dot_general(bo_full[rows, :], ratios, (((0,), (0,)), ((), ())),
                               preferred_element_type=F32)

    mixed = back_project(ring, core)
    for c in to_twin:
        c.wait_recv()
    mixed = (mixed + back_project(ring_twin, 1 - core)).astype(BF)
    raw = dot_nt(mixed, bi_full[...])
    for o in range(OWNERS):
        raw_buf[o] = raw[:, o * LANES:(o + 1) * LANES]
    squares = jnp.sum(jnp.sum(raw * raw, axis=0, keepdims=True), axis=1, keepdims=True)
    mean_sq = squares * (1.0 / (channels * 2 * channels))
    update_ref[...] = raw_buf[owner] / jnp.sqrt(mean_sq + 1e-06)
    for c in sum_copies + list(ring_copies.values()) + to_twin:
        c.wait_send()


def copy_kernel(a_ref, b_ref, a_out, b_out, sems):
    first = pltpu.make_async_copy(a_ref, a_out, sems.at[0])
    second = pltpu.make_async_copy(b_ref, b_out, sems.at[1])
    first.start()
    second.start()
    first.wait()
    second.wait()


def body(
    block_input_rows, spin_values, conv_weight, conv_bias, readout, energies, basis_out, basis_in
):
    samples, sites, channels = block_input_rows.shape
    vmem = pl.BlockSpec(memory_space=pltpu.VMEM)
    dma = pltpu.SemaphoreType.DMA
    result = jax.ShapeDtypeStruct((channels, LANES), F32)
    pairs = pl.pallas_call(
        kernel,
        out_shape=(result, result),
        in_specs=[pl.BlockSpec(memory_space=pl.ANY), vmem, vmem, vmem, vmem,
                  pl.BlockSpec(memory_space=pltpu.SMEM), vmem, vmem],
        out_specs=(vmem, vmem),
        scratch_shapes=[
            pltpu.VMEM((samples, sites + DILATION_STEP, channels), BF),
            pltpu.VMEM((channels, sites), BF),
            pltpu.VMEM((channels, sites), BF),
            pltpu.VMEM((samples, channels, 2 * channels), BF),
            pltpu.VMEM((samples, channels, 2 * channels), BF),
            pltpu.VMEM((channels, channels), BF),
            pltpu.VMEM((2 * channels, 2 * channels), BF),
            pltpu.VMEM((channels, LANES), F32),
            pltpu.VMEM((channels, LANES), F32),
            pltpu.VMEM((channels + 16, 2 * channels), BF),
            pltpu.VMEM((4, 8, LANES), F32),
            pltpu.VMEM((19, 8, LANES), F32),
            pltpu.VMEM((OWNERS, GROUPS, 16, LANES), BF),
            pltpu.VMEM((OWNERS, GROUPS, 16, LANES), BF),
            pltpu.VMEM((OWNERS, GROUPS, 16, LANES), F32),
            pltpu.VMEM((OWNERS, GROUPS, 16, LANES), BF),
            pltpu.VMEM((len(OFFSETS), 16, LANES), BF),
            pltpu.VMEM((OWNERS, GROUPS, 16, LANES), BF),
            pltpu.VMEM((OWNERS, GROUPS, 16, LANES), BF),
            pltpu.VMEM((OWNERS, channels, LANES), F32),
            dma((samples,)),
            dma((9,)), dma((9,)),
            dma((19,)), dma((19,)),
            dma(()), dma(()),
            dma((len(OFFSETS),)), dma((len(OFFSETS),)),
            dma((len(OFFSETS),)), dma((len(OFFSETS),)),
            dma((4,)), dma((4,)),
        ],
        compiler_params=pltpu.CompilerParams(
            collective_id=0, has_side_effects=True, vmem_limit_bytes=56 << 20),
    )(
        block_input_rows, spin_values, conv_weight,
        conv_bias.reshape(1, channels), readout.reshape(1, channels), energies,
        basis_out.T, basis_in,
    )
    anywhere = pl.BlockSpec(memory_space=pl.ANY)
    return pl.pallas_call(
        copy_kernel,
        out_shape=(result, result),
        in_specs=[anywhere, anywhere],
        out_specs=(anywhere, anywhere),
        scratch_shapes=[dma((2,))],
    )(*pairs)


def solution(mesh):
    in_specs = (
        P(("walker", "owner"), None, None),
        P(("walker", "owner"), None),
        P(),
        P(),
        P(),
        P(("walker", "owner")),
        P(None, "owner"),
        P(None, "owner"),
    )
    out_specs = (P(None, "owner"), P(None, "owner"))
    return jax.shard_map(body, mesh=mesh, in_specs=in_specs, out_specs=out_specs, check_vma=False)
```

time: 61.8 us -> 54.9 us (0.89)
  Pallas kernels: 57.9 us -> 54.2 us
  local copies, waits for them, and re-layouts: 3.14 us -> 0 us
    pallas_call x1 -> x2, Pallas kernels: 57.9 us -> 54.2 us  [the longest x1 45.1 us: body(): pl.pallas_call(kernel, out_shape=(result, result), in_specs=[pl.BlockSpec...]
    unnamed x2 -> x0, local copies, waits for them, and re-layouts: 3.14 us -> none
where the time goes in v2:
time: 54.9 us; the launch traced here: 54.8 us
  Pallas kernels  54.2 us (99%)
  between operations  0.64 us (1%)
    pallas_call x1, Pallas kernels, body(): pl.pallas_call(kernel, out_shape=(result, result), in_specs=[pl.BlockSpec...  45.1 us
    pallas_call x1, Pallas kernels, body(): pl.pallas_call(copy_kernel, out_shape=(result, result), in_specs=[anywher...  9.06 us

profile of v2, /device:TPU:1, one launch (start us, length us, event | category | flops | bytes accessed | tf_op | source)
XLA Modules:
  0.0 54.8 jit_solution(3332949708107112622)
XLA Ops:
  0.6 45.1 %shard_map.95 = (f32[256,128]{1,0:T(8,128)}, f32[256,128]{1,0:T(8,128)}) custom-call(bf16[16,1024,256]{2,1,0:T(8,128)(2,1)} %x_hbm.1, s32[16,1024]{1,0:T(8,128)} %spin_ref.1, bf16[256,512]{1,0:T(8,128)(2,1)} %w_ref.1, f32[1,256]{1,0:T(1,128)} %bitcast.4, f32[1,256]{1,0:T(1,128)} %bitcast.5, f32[16]{0:T(128)} %e_ref.1, bf16[64,256]{1,0:T(8,128)(2,1)} %bitcast.3, ...), custom_call_target="tpu_custom_call" | custom-call | tf_op jit(solution)/shard_map/pallas_call | solution.py:311
  45.7 9.1 %shard_map.96 = (f32[256,128]{1,0:T(8,128)}, f32[256,128]{1,0:T(8,128)}) custom-call(f32[256,128]{1,0:T(8,128)} %get-tuple-element.4.a_ref, f32[256,128]{1,0:T(8,128)} %get-tuple-element.5.b_ref), custom_call_target="tpu_custom_call" | custom-call | tf_op jit(solution)/shard_map/pallas_call | solution.py:354

commit v3 on v2

v3 whole, which is shorter than its diff:
```python
import jax
import jax.numpy as jnp
from jax import lax
from jax.experimental import pallas as pl
from jax.experimental.pallas import tpu as pltpu
from jax.sharding import PartitionSpec as P

DILATION_STEP = 16
DAMPING = 0.01
BF = jnp.bfloat16
F32 = jnp.float32
MESH = pl.DeviceIdType.MESH

GROUPS = 16
OWNERS = 4
LANES = 128


def dot_nt(a, b):
    return lax.dot_general(a, b, (((1,), (1,)), ((), ())), preferred_element_type=F32)


def dot_nn(a, b):
    return jnp.dot(a, b, preferred_element_type=F32)


def wide(value, count):
    return jnp.concatenate([value] * count, axis=1) if count > 1 else value


OFFSETS = sorted(
    [(dx, dy, dz) for dx in range(4) for dy in range(4) for dz in range(4)][1:],
    key=lambda step: -sum(min(d, 4 - d) for d in step),
)


def kernel(
    x_hbm, spin_hbm, w_hbm, bias_hbm, readout_hbm, e_ref, bo_hbm, bi_hbm,
    stats_ref, update_ref,
    xbuf, spin_ref, bias_ref, readout_ref, back_a, back_b, grads, halves, bo_full, bo_used,
    bo_turned, bi_full, bias_col, read_col, weight,
    e_out, e_in, core_out, core_in, own, sum_out, sum_in, swap_out, swap_in,
    ring, moments_ring, raw_buf,
    x_sem, in_sem, send_sem, recv_sem,
):
    samples, sites, channels = x_hbm.shape
    pad = DILATION_STEP
    total_samples = samples * 128
    walker = lax.axis_index("walker")
    owner = lax.axis_index("owner")
    core = lax.rem(walker, 2)
    group = walker // 2
    gx, gz = group // 4, lax.rem(group, 4)
    xs = [gx * 4] + [lax.rem(gx + d, 4) * 4 for d in (1, 2, 3)]
    zs = [gz] + [lax.rem(gz + d, 4) for d in (1, 2, 3)]
    ys = [owner] + [lax.rem(owner + d, 4) for d in (1, 2, 3)]

    def chip(dx, dy, dz):
        return ((xs[dx] + zs[dz]) * 2 + core, ys[dy])

    twin = (group * 2 + (1 - core), owner)
    across = [((gx * 4 + gz) * 2 + 1 - core, ys[d]) for d in (1, 2, 3)]
    line_x = [chip(d, 0, 0) for d in (1, 2, 3)]
    line_y = [chip(0, d, 0) for d in (1, 2, 3)] + across + [twin]
    line_z = [chip(0, 0, d) for d in (1, 2, 3)]
    peers = line_x + line_z + line_y

    barrier = pltpu.get_barrier_semaphore()
    for peer in peers:
        pl.semaphore_signal(barrier, inc=1, device_id=peer, device_id_type=MESH)

    def load(j):
        pair = pl.ds(2 * j, 2)
        return pltpu.make_async_copy(
            x_hbm.at[pair], xbuf.at[pair, pl.ds(pad, sites), :], x_sem.at[j])

    own_rows = pl.ds(pl.multiple_of(owner * 64, 64), 64)
    own_cols = pl.ds(pl.multiple_of(owner * LANES, LANES), LANES)
    inputs = [
        pltpu.make_async_copy(w_hbm, weight.at[pl.ds(0, channels), :], in_sem.at[0]),
        pltpu.make_async_copy(bias_hbm, bias_ref, in_sem.at[1]),
        pltpu.make_async_copy(readout_hbm, readout_ref, in_sem.at[2]),
        pltpu.make_async_copy(spin_hbm, spin_ref, in_sem.at[3]),
    ]
    bases = [
        pltpu.make_async_copy(bo_hbm, bo_full.at[own_rows, :], in_sem.at[4]),
        pltpu.make_async_copy(bi_hbm, bi_full.at[:, own_cols], in_sem.at[5]),
    ]
    for c in inputs[:3]:
        c.start()
    load(0).start()
    inputs[3].start()
    for j in range(1, samples // 2):
        load(j).start()
    for c in bases:
        c.start()
    for i in range(samples):
        xbuf[i, 0:pad, :] = jnp.zeros((pad, channels), BF)
    for c in inputs:
        c.wait()

    def send(src, dst, ssem, rsem, peer):
        return pltpu.make_async_remote_copy(
            src_ref=src, dst_ref=dst, send_sem=ssem, recv_sem=rsem,
            device_id=peer, device_id_type=MESH,
        )

    bias_col[...] = jnp.broadcast_to(bias_ref[...], (LANES, channels)).T
    read_col[...] = jnp.broadcast_to(readout_ref[...], (LANES, channels)).T
    r = readout_ref[...]
    hi = r.astype(BF).astype(F32)
    mid = (r - hi).astype(BF).astype(F32)
    low = r - hi - mid
    row = lax.broadcasted_iota(jnp.int32, (16, channels), 0)
    spread = jnp.where(row == 0, hi, jnp.where(row == 1, mid, jnp.where(row == 2, low, 0.0)))
    weight[channels:, :channels] = jnp.zeros((16, channels), BF)
    weight[channels:, channels:] = spread.astype(BF)

    bi_half = pl.ds(pl.multiple_of(core * channels, channels), channels)

    def bo_copies():
        part = bo_full.at[own_rows, :]
        return [send(part, part, send_sem.at[0], recv_sem.at[0], chip(0, d, 0))
                for d in (1, 2, 3)]

    def bi_copies():
        part = bi_full.at[bi_half, own_cols]
        return [send(part, part, send_sem.at[1], recv_sem.at[1], chip(0, d, 0))
                for d in (1, 2, 3)]

    def bi_relays():
        out = []
        for d in (1, 2, 3):
            cols = pl.ds(pl.multiple_of(ys[d] * LANES, LANES), LANES)
            part = bi_full.at[bi_half, cols]
            out.append(send(part, part, send_sem.at[2], recv_sem.at[2], twin))
        return out

    bo_all = bo_full.at[pl.ds(0, 192), :]
    bi_all = bi_full.at[pl.ds(0, channels), pl.ds(0, 3 * LANES)]

    def finish(k, part):
        both = send(part, part, send_sem.at[k], recv_sem.at[k], twin)
        both.wait_recv()
        both.wait_send()

    e_sum = e_ref[0]
    for i in range(1, samples):
        e_sum = e_sum + e_ref[i]
    e_out[0] = jnp.full((8, LANES), e_sum, F32)
    stages = [line_y, line_x, line_z]
    first_slot = [0, 7, 10]

    def energy_start(stage):
        for k, peer in enumerate(stages[stage]):
            send(e_out.at[stage], e_in.at[first_slot[stage] + k], send_sem.at[3 + stage],
                 recv_sem.at[3 + stage], peer).start()

    def energy_finish(stage):
        slots = range(first_slot[stage], first_slot[stage] + len(stages[stage]))
        finish(3 + stage, e_in.at[pl.ds(slots[0], len(slots))])
        total = e_out[stage]
        for k in slots:
            total = total + e_in[k]
        e_out[stage + 1] = total

    chunk = 256

    def forward(i, back):
        for c in range(sites // chunk):
            lo = c * chunk
            x_prev = xbuf[i, lo:lo + chunk, :]
            x_now = xbuf[i, lo + pad:lo + pad + chunk, :]
            out = dot_nt(weight[...], jnp.concatenate([x_prev, x_now], axis=1))
            act = jnp.tanh(out[:channels] + wide(bias_col[...], chunk // LANES))
            logit = jnp.sum(act * wide(read_col[...], chunk // LANES), axis=0, keepdims=True)
            logit = logit + jnp.sum(out[channels:], axis=0, keepdims=True)
            target = spin_ref[pl.ds(i, 1), lo:lo + chunk].astype(F32)
            signal = 0.5 * (target - jax.nn.sigmoid(logit))
            back[:, lo:lo + chunk] = (signal * (1.0 - act * act)).astype(BF)

    def gradient(i, back):
        scale = wide(read_col[...], channels // LANES)
        b = back[...]
        grads[i, :, :channels] = (dot_nn(b, xbuf[i, :sites, :]) * scale).astype(BF)
        grads[i, :, channels:] = (dot_nn(b, xbuf[i, pad:, :]) * scale).astype(BF)

    @pl.loop(0, samples // 2)
    def _(j):
        @pl.when(j == 2)
        def _():
            pl.semaphore_wait(barrier, len(peers))
            energy_start(0)
            for c in bases:
                c.wait()
            for c in bo_copies() + bi_copies():
                c.start()

        @pl.when(j == 5)
        def _():
            energy_finish(0)
            energy_start(1)

        load(j).wait()
        forward(2 * j, back_a)
        forward(2 * j + 1, back_b)
        gradient(2 * j, back_a)
        gradient(2 * j + 1, back_b)

    energy_finish(1)
    energy_start(2)
    finish(0, bo_all)
    finish(1, bi_all)
    for c in bi_relays():
        c.start()

    blocks = bo_full[...].astype(F32).reshape(GROUPS, 2, 8, channels)
    bo_used[...] = jnp.concatenate(
        [blocks[:, k].reshape(128, channels) for k in range(2)], axis=0).astype(BF)

    @pl.loop(0, samples // 8)
    def _(j):
        for u in range(8):
            halves[8 * j + u] = dot_nn(bo_used[...], grads[8 * j + u]).astype(BF)

    energy_finish(2)
    finish(2, bi_all)

    e_mean = jnp.broadcast_to(e_out[3][0:1, :], (64, LANES)) * (1.0 / total_samples)

    def project(first, tile):
        q, m = tile // 2, tile % 2
        rows = pl.ds(pl.multiple_of(first + q * 64, 64), 64)
        lhs = halves[:, rows, :].reshape(samples * 64, 2 * channels)
        p = dot_nn(lhs, bi_full[:, m * 256:(m + 1) * 256])
        squares = jnp.zeros((64, 256), F32)
        weighted = jnp.zeros((64, 256), F32)
        for n in range(samples):
            pn = p[n * 64:(n + 1) * 64]
            squares = squares + pn * pn
            weighted = weighted + pn * wide(e_ref[n] - e_mean, 2)
        out = []
        for k in range(2):
            cols = slice(k * LANES, (k + 1) * LANES)
            out.append((2 * m + k, q * 8, jnp.concatenate(
                [squares[:, cols].reshape(8, 8, LANES), weighted[:, cols].reshape(8, 8, LANES)],
                axis=1)))
        return out

    for tile in range(4):
        for o, g, block in project((1 - core) * 128, tile):
            core_out[o, g:g + 8] = block.astype(BF)
    core_copy = send(core_out, core_in, send_sem.at[6], recv_sem.at[6], twin)
    core_copy.start()
    for tile in range(4):
        for o, g, block in project(core * 128, tile):
            own[o, g:g + 8] = block
    core_copy.wait()

    sum_out[...] = (own[...] + core_in[...].astype(F32)).astype(BF)
    for k, (dx, dy, dz) in enumerate(OFFSETS):
        send(sum_out.at[ys[dy], xs[dx] + zs[dz]], sum_in.at[k], send_sem.at[7],
             recv_sem.at[7], chip(dx, dy, dz)).start()
    bo_turned[...] = bo_full[...].T
    final = sum_out[owner, group].astype(F32)
    finish(7, sum_in)
    for k in range(len(OFFSETS)):
        final = final + sum_in[k].astype(F32)

    final = final * (1.0 / total_samples)
    moments = final[0:8]
    ratio = final[8:16] / (moments + DAMPING)
    swap_out[...] = jnp.concatenate([ratio, moments], axis=0)
    swap = send(swap_out, swap_in, send_sem.at[8], recv_sem.at[8], twin)
    swap.start()
    swap.wait()
    mine, other = swap_out[...], swap_in[...]
    upper = jnp.where(core == 0, mine, other)
    lower = jnp.where(core == 0, other, mine)
    ring[owner, group] = jnp.concatenate([upper[0:8], lower[0:8]], axis=0).astype(BF)
    moments_ring[group] = jnp.concatenate([upper[8:16], lower[8:16]], axis=0).astype(BF)
    tile = ring.at[owner, group]
    for dx, dy, dz in OFFSETS:
        send(tile, tile, send_sem.at[9], recv_sem.at[9], chip(dx, dy, dz)).start()
    tile = moments_ring.at[group]
    for dx, dy, dz in OFFSETS:
        if dy == 0:
            send(tile, tile, send_sem.at[10], recv_sem.at[10], chip(dx, dy, dz)).start()
    ring_all = send(sum_in, sum_in, send_sem.at[9], recv_sem.at[9], twin)
    stat_all = moments_ring.at[pl.ds(0, GROUPS - 1)]
    stat_all = send(stat_all, stat_all, send_sem.at[10], recv_sem.at[10], twin)
    ring_all.wait_recv()

    ratios = jnp.concatenate(
        [ring[o].reshape(channels, LANES) for o in range(OWNERS)], axis=1)
    mixed = dot_nn(bo_turned[...], ratios).astype(BF)
    raw = dot_nt(mixed, bi_full[...])
    for o in range(OWNERS):
        raw_buf[o] = raw[:, o * LANES:(o + 1) * LANES]
    squares = jnp.sum(jnp.sum(raw * raw, axis=0, keepdims=True), axis=1, keepdims=True)
    mean_sq = squares * (1.0 / (channels * 2 * channels))
    update_ref[...] = raw_buf[owner] / jnp.sqrt(mean_sq + 1e-06)
    stat_all.wait_recv()
    stats_ref[...] = moments_ring[...].reshape(channels, LANES).astype(F32)
    ring_all.wait_send()
    stat_all.wait_send()


def copy_kernel(a_ref, b_ref, a_out, b_out):
    a_out[...] = a_ref[...]
    b_out[...] = b_ref[...]


def body(
    block_input_rows, spin_values, conv_weight, conv_bias, readout, energies, basis_out, basis_in
):
    samples, sites, channels = block_input_rows.shape
    vmem = pl.BlockSpec(memory_space=pltpu.VMEM)
    anywhere = pl.BlockSpec(memory_space=pl.ANY)
    dma = pltpu.SemaphoreType.DMA
    result = jax.ShapeDtypeStruct((channels, LANES), F32)
    pairs = pl.pallas_call(
        kernel,
        out_shape=(result, result),
        in_specs=[anywhere] * 5 + [pl.BlockSpec(memory_space=pltpu.SMEM)] + [anywhere] * 2,
        out_specs=(vmem, vmem),
        scratch_shapes=[
            pltpu.VMEM((samples, sites + DILATION_STEP, channels), BF),
            pltpu.VMEM((samples, sites), jnp.int32),
            pltpu.VMEM((1, channels), F32),
            pltpu.VMEM((1, channels), F32),
            pltpu.VMEM((channels, sites), BF),
            pltpu.VMEM((channels, sites), BF),
            pltpu.VMEM((samples, channels, 2 * channels), BF),
            pltpu.VMEM((samples, channels, 2 * channels), BF),
            pltpu.VMEM((channels, channels), BF),
            pltpu.VMEM((channels, channels), BF),
            pltpu.VMEM((channels, channels), BF),
            pltpu.VMEM((2 * channels, 2 * channels), BF),
            pltpu.VMEM((channels, LANES), F32),
            pltpu.VMEM((channels, LANES), F32),
            pltpu.VMEM((channels + 16, 2 * channels), BF),
            pltpu.VMEM((4, 8, LANES), F32),
            pltpu.VMEM((13, 8, LANES), F32),
            pltpu.VMEM((OWNERS, GROUPS, 16, LANES), BF),
            pltpu.VMEM((OWNERS, GROUPS, 16, LANES), BF),
            pltpu.VMEM((OWNERS, GROUPS, 16, LANES), F32),
            pltpu.VMEM((OWNERS, GROUPS, 16, LANES), BF),
            pltpu.VMEM((len(OFFSETS), 16, LANES), BF),
            pltpu.VMEM((16, LANES), F32),
            pltpu.VMEM((16, LANES), F32),
            pltpu.VMEM((OWNERS, GROUPS, 16, LANES), BF),
            pltpu.VMEM((GROUPS, 16, LANES), BF),
            pltpu.VMEM((OWNERS, channels, LANES), F32),
            dma((samples // 2,)), dma((6,)), dma((11,)), dma((11,)),
        ],
        compiler_params=pltpu.CompilerParams(
            collective_id=0, has_side_effects=True, vmem_limit_bytes=56 << 20),
    )(
        block_input_rows, spin_values, conv_weight,
        conv_bias.reshape(1, channels), readout.reshape(1, channels), energies,
        basis_out.T, basis_in,
    )
    return pl.pallas_call(
        copy_kernel,
        out_shape=(result, result),
        in_specs=[vmem, vmem],
        out_specs=(vmem, vmem),
    )(*pairs)


def solution(mesh):
    in_specs = (
        P(("walker", "owner"), None, None),
        P(("walker", "owner"), None),
        P(),
        P(),
        P(),
        P(("walker", "owner")),
        P(None, "owner"),
        P(None, "owner"),
    )
    out_specs = (P(None, "owner"), P(None, "owner"))
    return jax.shard_map(body, mesh=mesh, in_specs=in_specs, out_specs=out_specs, check_vma=False)
```

time: 54.9 us -> 45 us (0.82)
  Pallas kernels: 54.2 us -> 44.3 us
    pallas_call x2, Pallas kernels: 54.2 us -> 44.3 us  [the longest x1 42.6 us: body(): pl.pallas_call(kernel, out_shape=(result, result), in_specs=[anywhere] *...]
where the time goes in v3:
time: 45 us; the launch traced here: 44.9 us
  Pallas kernels  44.3 us (98%)
  between operations  0.64 us (1%)
    pallas_call x1, Pallas kernels, body(): pl.pallas_call(kernel, out_shape=(result, result), in_specs=[anywhere] *...  42.6 us
    pallas_call x1, Pallas kernels, body(): pl.pallas_call(copy_kernel, out_shape=(result, result), in_specs=[vmem, v...  1.68 us

profile of v3, /device:TPU:1, one launch (start us, length us, event | category | flops | bytes accessed | tf_op | source)
XLA Modules:
  0.0 44.9 jit_solution(13232465240769166269)
XLA Ops:
  0.6 42.6 %shard_map.95 = (f32[256,128]{1,0:T(8,128)}, f32[256,128]{1,0:T(8,128)}) custom-call(bf16[16,1024,256]{2,1,0:T(8,128)(2,1)} %x_hbm.1, s32[16,1024]{1,0:T(8,128)} %spin_hbm.1, bf16[256,512]{1,0:T(8,128)(2,1)} %w_hbm.1, f32[1,256]{1,0:T(1,128)} %bitcast.4, f32[1,256]{1,0:T(1,128)} %bitcast.5, f32[16]{0:T(128)} %e_ref.1, bf16[64,256]{1,0:T(8,128)(2,1)} %bitcast.3, ...), custom_call_target="tpu_custom_call" | custom-call | tf_op jit(solution)/shard_map/pallas_call | solution.py:322
  43.2 1.7 %shard_map.96 = (f32[256,128]{1,0:T(8,128)}, f32[256,128]{1,0:T(8,128)}) custom-call(f32[256,128]{1,0:T(8,128)} %get-tuple-element.4.a_ref, f32[256,128]{1,0:T(8,128)} %get-tuple-element.5.b_ref), custom_call_target="tpu_custom_call" | custom-call | tf_op jit(solution)/shard_map/pallas_call | solution.py:364

commit v4 on v3

--- a/solution.py
+++ b/solution.py
@@ -86,18 +86,17 @@
         pltpu.make_async_copy(bo_hbm, bo_full.at[own_rows, :], in_sem.at[4]),
         pltpu.make_async_copy(bi_hbm, bi_full.at[:, own_cols], in_sem.at[5]),
     ]
-    for c in inputs[:3]:
-        c.start()
     load(0).start()
-    inputs[3].start()
-    for j in range(1, samples // 2):
-        load(j).start()
-    for c in bases:
+    for c in inputs:
         c.start()
     for i in range(samples):
         xbuf[i, 0:pad, :] = jnp.zeros((pad, channels), BF)
     for c in inputs:
         c.wait()
+    for j in range(1, samples // 2):
+        load(j).start()
+    for c in bases:
+        c.start()
 
     def send(src, dst, ssem, rsem, peer):
         return pltpu.make_async_remote_copy(
@@ -196,10 +195,21 @@
             for c in bo_copies() + bi_copies():
                 c.start()
 
-        @pl.when(j == 5)
+        @pl.when(j == 4)
         def _():
             energy_finish(0)
             energy_start(1)
+
+        @pl.when(j == 6)
+        def _():
+            energy_finish(1)
+            energy_start(2)
+
+        @pl.when(j == 7)
+        def _():
+            finish(1, bi_all)
+            for c in bi_relays():
+                c.start()
 
         load(j).wait()
         forward(2 * j, back_a)
@@ -207,12 +217,7 @@
         gradient(2 * j, back_a)
         gradient(2 * j + 1, back_b)
 
-    energy_finish(1)
-    energy_start(2)
     finish(0, bo_all)
-    finish(1, bi_all)
-    for c in bi_relays():
-        c.start()
 
     blocks = bo_full[...].astype(F32).reshape(GROUPS, 2, 8, channels)
     bo_used[...] = jnp.concatenate(

time: 45 us -> 43.1 us (0.958)
  Pallas kernels: 44.3 us -> 42.3 us
    pallas_call x1, Pallas kernels: 42.6 us -> 40.6 us  [body(): pl.pallas_call(kernel, out_shape=(result, result), in_specs=[anywhere] *...]
where the time goes in v4:
time: 43.1 us; the launch traced here: 42.9 us
  Pallas kernels  42.3 us (98%)
  between operations  0.64 us (1%)
    pallas_call x1, Pallas kernels, body(): pl.pallas_call(kernel, out_shape=(result, result), in_specs=[anywhere] *...  40.6 us
    pallas_call x1, Pallas kernels, body(): pl.pallas_call(copy_kernel, out_shape=(result, result), in_specs=[vmem, v...  1.68 us

profile of v4, /device:TPU:1, one launch (start us, length us, event | category | flops | bytes accessed | tf_op | source)
XLA Modules:
  0.0 42.9 jit_solution(9694475958483813079)
XLA Ops:
  0.6 40.6 %shard_map.95 = (f32[256,128]{1,0:T(8,128)}, f32[256,128]{1,0:T(8,128)}) custom-call(bf16[16,1024,256]{2,1,0:T(8,128)(2,1)} %x_hbm.1, s32[16,1024]{1,0:T(8,128)} %spin_hbm.1, bf16[256,512]{1,0:T(8,128)(2,1)} %w_hbm.1, f32[1,256]{1,0:T(1,128)} %bitcast.4, f32[1,256]{1,0:T(1,128)} %bitcast.5, f32[16]{0:T(128)} %e_ref.1, bf16[64,256]{1,0:T(8,128)(2,1)} %bitcast.3, ...), custom_call_target="tpu_custom_call" | custom-call | tf_op jit(solution)/shard_map/pallas_call | solution.py:327
  41.2 1.7 %shard_map.96 = (f32[256,128]{1,0:T(8,128)}, f32[256,128]{1,0:T(8,128)}) custom-call(f32[256,128]{1,0:T(8,128)} %get-tuple-element.4.a_ref, f32[256,128]{1,0:T(8,128)} %get-tuple-element.5.b_ref), custom_call_target="tpu_custom_call" | custom-call | tf_op jit(solution)/shard_map/pallas_call | solution.py:369

commit v5 on v3

--- a/solution.py
+++ b/solution.py
@@ -39,7 +39,7 @@
     stats_ref, update_ref,
     xbuf, spin_ref, bias_ref, readout_ref, back_a, back_b, grads, halves, bo_full, bo_used,
     bo_turned, bi_full, bias_col, read_col, weight,
-    e_out, e_in, core_out, core_in, own, sum_out, sum_in, swap_out, swap_in,
+    e_out, e_in, core_out, core_in, own, plain_out, plain_in, own_plain, sum_out, sum_in, swap_out, swap_in,
     ring, moments_ring, raw_buf,
     x_sem, in_sem, send_sem, recv_sem,
 ):
@@ -86,18 +86,17 @@
         pltpu.make_async_copy(bo_hbm, bo_full.at[own_rows, :], in_sem.at[4]),
         pltpu.make_async_copy(bi_hbm, bi_full.at[:, own_cols], in_sem.at[5]),
     ]
-    for c in inputs[:3]:
-        c.start()
     load(0).start()
-    inputs[3].start()
-    for j in range(1, samples // 2):
-        load(j).start()
-    for c in bases:
+    for c in inputs:
         c.start()
     for i in range(samples):
         xbuf[i, 0:pad, :] = jnp.zeros((pad, channels), BF)
     for c in inputs:
         c.wait()
+    for j in range(1, samples // 2):
+        load(j).start()
+    for c in bases:
+        c.start()
 
     def send(src, dst, ssem, rsem, peer):
         return pltpu.make_async_remote_copy(
@@ -223,10 +222,9 @@
         for u in range(8):
             halves[8 * j + u] = dot_nn(bo_used[...], grads[8 * j + u]).astype(BF)
 
-    energy_finish(2)
     finish(2, bi_all)
 
-    e_mean = jnp.broadcast_to(e_out[3][0:1, :], (64, LANES)) * (1.0 / total_samples)
+    e_local = e_sum * (1.0 / samples)
 
     def project(first, tile):
         q, m = tile // 2, tile % 2
@@ -235,29 +233,43 @@
         p = dot_nn(lhs, bi_full[:, m * 256:(m + 1) * 256])
         squares = jnp.zeros((64, 256), F32)
         weighted = jnp.zeros((64, 256), F32)
+        plain = jnp.zeros((64, 256), F32)
         for n in range(samples):
             pn = p[n * 64:(n + 1) * 64]
             squares = squares + pn * pn
-            weighted = weighted + pn * wide(e_ref[n] - e_mean, 2)
+            weighted = weighted + pn * (e_ref[n] - e_local)
+            plain = plain + pn
         out = []
         for k in range(2):
             cols = slice(k * LANES, (k + 1) * LANES)
-            out.append((2 * m + k, q * 8, jnp.concatenate(
-                [squares[:, cols].reshape(8, 8, LANES), weighted[:, cols].reshape(8, 8, LANES)],
-                axis=1)))
+            parts = [v[:, cols].reshape(8, 8, LANES) for v in (squares, weighted)]
+            out.append((2 * m + k, q, jnp.concatenate(parts, axis=1), plain[:, cols]))
         return out
 
     for tile in range(4):
-        for o, g, block in project((1 - core) * 128, tile):
-            core_out[o, g:g + 8] = block.astype(BF)
+        for o, q, block, plain in project((1 - core) * 128, tile):
+            core_out[o, q * 8:q * 8 + 8] = block.astype(BF)
+            plain_out[o, q * 64:q * 64 + 64] = plain.astype(BF)
     core_copy = send(core_out, core_in, send_sem.at[6], recv_sem.at[6], twin)
     core_copy.start()
+    plain_copy = send(plain_out, plain_in, send_sem.at[11], recv_sem.at[11], twin)
+    plain_copy.start()
     for tile in range(4):
-        for o, g, block in project(core * 128, tile):
-            own[o, g:g + 8] = block
+        for o, q, block, plain in project(core * 128, tile):
+            own[o, q * 8:q * 8 + 8] = block
+            own_plain[o, q * 64:q * 64 + 64] = plain
+    energy_finish(2)
+    e_mean = e_out[3][0:1, :] * (1.0 / total_samples)
+    here = e_out[0][0:1, :] * (1.0 / samples) - e_mean
+    there = e_in[6][0:1, :] * (1.0 / samples) - e_mean
     core_copy.wait()
-
-    sum_out[...] = (own[...] + core_in[...].astype(F32)).astype(BF)
+    plain_copy.wait()
+
+    for o in range(OWNERS):
+        both = own[o] + core_in[o].astype(F32)
+        shift = own_plain[o] * here + plain_in[o].astype(F32) * there
+        sum_out[o] = jnp.concatenate(
+            [both[:, :8], both[:, 8:] + shift.reshape(GROUPS, 8, LANES)], axis=1).astype(BF)
     for k, (dx, dy, dz) in enumerate(OFFSETS):
         send(sum_out.at[ys[dy], xs[dx] + zs[dz]], sum_in.at[k], send_sem.at[7],
              recv_sem.at[7], chip(dx, dy, dz)).start()
@@ -345,6 +357,9 @@
             pltpu.VMEM((OWNERS, GROUPS, 16, LANES), BF),
             pltpu.VMEM((OWNERS, GROUPS, 16, LANES), BF),
             pltpu.VMEM((OWNERS, GROUPS, 16, LANES), F32),
+            pltpu.VMEM((OWNERS, channels // 2, LANES), BF),
+            pltpu.VMEM((OWNERS, channels // 2, LANES), BF),
+            pltpu.VMEM((OWNERS, channels // 2, LANES), F32),
             pltpu.VMEM((OWNERS, GROUPS, 16, LANES), BF),
             pltpu.VMEM((len(OFFSETS), 16, LANES), BF),
             pltpu.VMEM((16, LANES), F32),
@@ -352,7 +367,7 @@
             pltpu.VMEM((OWNERS, GROUPS, 16, LANES), BF),
             pltpu.VMEM((GROUPS, 16, LANES), BF),
             pltpu.VMEM((OWNERS, channels, LANES), F32),
-            dma((samples // 2,)), dma((6,)), dma((11,)), dma((11,)),
+            dma((samples // 2,)), dma((6,)), dma((12,)), dma((12,)),
         ],
         compiler_params=pltpu.CompilerParams(
             collective_id=0, has_side_effects=True, vmem_limit_bytes=56 << 20),

time: 45 us -> 41.8 us (0.929)
  Pallas kernels: 44.3 us -> 41 us
    pallas_call x1, Pallas kernels: 42.6 us -> 39.3 us  [body(): pl.pallas_call(kernel, out_shape=(result, result), in_specs=[anywhere] *...]
where the time goes in v5:
time: 41.8 us; the launch traced here: 41.7 us
  Pallas kernels  41 us (98%)
  between operations  0.64 us (2%)
    pallas_call x1, Pallas kernels, body(): pl.pallas_call(kernel, out_shape=(result, result), in_specs=[anywhere] *...  39.3 us
    pallas_call x1, Pallas kernels, body(): pl.pallas_call(copy_kernel, out_shape=(result, result), in_specs=[vmem, v...  1.68 us

profile of v5, /device:TPU:1, one launch (start us, length us, event | category | flops | bytes accessed | tf_op | source)
XLA Modules:
  0.0 41.7 jit_solution(6656131990022027215)
XLA Ops:
  0.6 39.3 %shard_map.95 = (f32[256,128]{1,0:T(8,128)}, f32[256,128]{1,0:T(8,128)}) custom-call(bf16[16,1024,256]{2,1,0:T(8,128)(2,1)} %x_hbm.1, s32[16,1024]{1,0:T(8,128)} %spin_hbm.1, bf16[256,512]{1,0:T(8,128)(2,1)} %w_hbm.1, f32[1,256]{1,0:T(1,128)} %bitcast.4, f32[1,256]{1,0:T(1,128)} %bitcast.5, f32[16]{0:T(128)} %e_ref.1, bf16[64,256]{1,0:T(8,128)(2,1)} %bitcast.3, ...), custom_call_target="tpu_custom_call" | custom-call | tf_op jit(solution)/shard_map/pallas_call | solution.py:334
  40.0 1.7 %shard_map.96 = (f32[256,128]{1,0:T(8,128)}, f32[256,128]{1,0:T(8,128)}) custom-call(f32[256,128]{1,0:T(8,128)} %get-tuple-element.4.a_ref, f32[256,128]{1,0:T(8,128)} %get-tuple-element.5.b_ref), custom_call_target="tpu_custom_call" | custom-call | tf_op jit(solution)/shard_map/pallas_call | solution.py:379

commit v6 on v5

--- a/solution.py
+++ b/solution.py
@@ -91,12 +91,8 @@
         c.start()
     for i in range(samples):
         xbuf[i, 0:pad, :] = jnp.zeros((pad, channels), BF)
-    for c in inputs:
+    for c in inputs[1:3]:
         c.wait()
-    for j in range(1, samples // 2):
-        load(j).start()
-    for c in bases:
-        c.start()
 
     def send(src, dst, ssem, rsem, peer):
         return pltpu.make_async_remote_copy(
@@ -114,6 +110,12 @@
     spread = jnp.where(row == 0, hi, jnp.where(row == 1, mid, jnp.where(row == 2, low, 0.0)))
     weight[channels:, :channels] = jnp.zeros((16, channels), BF)
     weight[channels:, channels:] = spread.astype(BF)
+    inputs[0].wait()
+    inputs[3].wait()
+    for j in range(1, samples // 2):
+        load(j).start()
+    for c in bases:
+        c.start()
 
     bi_half = pl.ds(pl.multiple_of(core * channels, channels), channels)
 
@@ -250,10 +252,14 @@
         for o, q, block, plain in project((1 - core) * 128, tile):
             core_out[o, q * 8:q * 8 + 8] = block.astype(BF)
             plain_out[o, q * 64:q * 64 + 64] = plain.astype(BF)
-    core_copy = send(core_out, core_in, send_sem.at[6], recv_sem.at[6], twin)
-    core_copy.start()
-    plain_copy = send(plain_out, plain_in, send_sem.at[11], recv_sem.at[11], twin)
-    plain_copy.start()
+        if tile % 2:
+            q = tile // 2
+            part = pl.ds(q * 8, 8)
+            send(core_out.at[:, part], core_in.at[:, part], send_sem.at[6], recv_sem.at[6],
+                 twin).start()
+            part = pl.ds(q * 64, 64)
+            send(plain_out.at[:, part], plain_in.at[:, part], send_sem.at[11], recv_sem.at[11],
+                 twin).start()
     for tile in range(4):
         for o, q, block, plain in project(core * 128, tile):
             own[o, q * 8:q * 8 + 8] = block
@@ -262,17 +268,19 @@
     e_mean = e_out[3][0:1, :] * (1.0 / total_samples)
     here = e_out[0][0:1, :] * (1.0 / samples) - e_mean
     there = e_in[6][0:1, :] * (1.0 / samples) - e_mean
-    core_copy.wait()
-    plain_copy.wait()
-
-    for o in range(OWNERS):
+    finish(6, core_in)
+    finish(11, plain_in)
+
+    for step in (2, 1, 3, 0):
+        o = ys[step]
         both = own[o] + core_in[o].astype(F32)
         shift = own_plain[o] * here + plain_in[o].astype(F32) * there
         sum_out[o] = jnp.concatenate(
             [both[:, :8], both[:, 8:] + shift.reshape(GROUPS, 8, LANES)], axis=1).astype(BF)
-    for k, (dx, dy, dz) in enumerate(OFFSETS):
-        send(sum_out.at[ys[dy], xs[dx] + zs[dz]], sum_in.at[k], send_sem.at[7],
-             recv_sem.at[7], chip(dx, dy, dz)).start()
+        for k, (dx, dy, dz) in enumerate(OFFSETS):
+            if dy == step:
+                send(sum_out.at[o, xs[dx] + zs[dz]], sum_in.at[k], send_sem.at[7],
+                     recv_sem.at[7], chip(dx, dy, dz)).start()
     bo_turned[...] = bo_full[...].T
     final = sum_out[owner, group].astype(F32)
     finish(7, sum_in)
@@ -331,9 +339,10 @@
     anywhere = pl.BlockSpec(memory_space=pl.ANY)
     dma = pltpu.SemaphoreType.DMA
     result = jax.ShapeDtypeStruct((channels, LANES), F32)
+    kept = pltpu.VMEM((channels, LANES), F32)
     pairs = pl.pallas_call(
         kernel,
-        out_shape=(result, result),
+        out_shape=(kept, kept),
         in_specs=[anywhere] * 5 + [pl.BlockSpec(memory_space=pltpu.SMEM)] + [anywhere] * 2,
         out_specs=(vmem, vmem),
         scratch_shapes=[
@@ -381,7 +390,7 @@
         out_shape=(result, result),
         in_specs=[vmem, vmem],
         out_specs=(vmem, vmem),
-    )(*pairs)
+    )(*[pltpu.with_memory_space_constraint(p, pltpu.VMEM) for p in pairs])
 
 
 def solution(mesh):

time: 41.8 us -> 40.1 us (0.959)
  Pallas kernels: 41 us -> 39.3 us
    pallas_call x1, Pallas kernels: 1.68 us -> 0.72 us  [body(): pl.pallas_call(copy_kernel, out_shape=(result, result), in_specs=[vmem, v...]
    pallas_call x1, Pallas kernels: 39.3 us -> 38.6 us  [body(): pl.pallas_call(kernel, out_shape=(kept, kept), in_specs=[anywhere] * 5 +...]
where the time goes in v6:
time: 40.1 us; the launch traced here: 39.9 us
  Pallas kernels  39.3 us (98%)
  between operations  0.64 us (2%)
    pallas_call x1, Pallas kernels, body(): pl.pallas_call(kernel, out_shape=(kept, kept), in_specs=[anywhere] * 5 +...  38.6 us

profile of v6, /device:TPU:1, one launch (start us, length us, event | category | flops | bytes accessed | tf_op | source)
XLA Modules:
  0.0 39.9 jit_solution(12403667572565056604)
XLA Ops:
  0.6 38.6 %shard_map.95 = (f32[256,128]{1,0:T(8,128)S(1)}, f32[256,128]{1,0:T(8,128)S(1)}) custom-call(bf16[16,1024,256]{2,1,0:T(8,128)(2,1)} %x_hbm.1, s32[16,1024]{1,0:T(8,128)} %spin_hbm.1, bf16[256,512]{1,0:T(8,128)(2,1)} %w_hbm.1, f32[1,256]{1,0:T(1,128)} %bitcast.4, f32[1,256]{1,0:T(1,128)} %bitcast.5, f32[16]{0:T(128)} %e_ref.1, bf16[64,256]{1,0:T(8,128)(2,1)} %bitcast.3, ...), custom_call_target="tpu_custom_call" | custom-call | tf_op jit(solution)/shard_map/pallas_call | solution.py:343
  39.2 0.7 %shard_map.96 = (f32[256,128]{1,0:T(8,128)}, f32[256,128]{1,0:T(8,128)}) custom-call(f32[256,128]{1,0:T(8,128)S(1)} %get-tuple-element.4.a_ref, f32[256,128]{1,0:T(8,128)S(1)} %get-tuple-element.5.b_ref), custom_call_target="tpu_custom_call" | custom-call | tf_op jit(solution)/shard_map/pallas_call | solution.py:388

commit v7 on v6

--- a/solution.py
+++ b/solution.py
@@ -326,9 +326,13 @@
     stat_all.wait_send()
 
 
-def copy_kernel(a_ref, b_ref, a_out, b_out):
-    a_out[...] = a_ref[...]
-    b_out[...] = b_ref[...]
+def copy_kernel(a_ref, b_ref, a_out, b_out, sems):
+    first = pltpu.make_async_copy(a_ref, a_out, sems.at[0])
+    second = pltpu.make_async_copy(b_ref, b_out, sems.at[1])
+    first.start()
+    second.start()
+    first.wait()
+    second.wait()
 
 
 def body(
@@ -389,7 +393,8 @@
         copy_kernel,
         out_shape=(result, result),
         in_specs=[vmem, vmem],
-        out_specs=(vmem, vmem),
+        out_specs=(anywhere, anywhere),
+        scratch_shapes=[dma((2,))],
     )(*[pltpu.with_memory_space_constraint(p, pltpu.VMEM) for p in pairs])
 
 

time: 40.1 us -> 40.1 us (level)
  no operation moved by 1% of the time
where the time goes in v7:
time: 40.1 us; the launch traced here: 39.9 us
  Pallas kernels  39.3 us (98%)
  between operations  0.64 us (2%)
    pallas_call x1, Pallas kernels, body(): pl.pallas_call(kernel, out_shape=(kept, kept), in_specs=[anywhere] * 5 +...  38.6 us

profile of v7, /device:TPU:1, one launch (start us, length us, event | category | flops | bytes accessed | tf_op | source)
XLA Modules:
  0.0 39.9 jit_solution(2268640824138905199)
XLA Ops:
  0.6 38.6 %shard_map.95 = (f32[256,128]{1,0:T(8,128)S(1)}, f32[256,128]{1,0:T(8,128)S(1)}) custom-call(bf16[16,1024,256]{2,1,0:T(8,128)(2,1)} %x_hbm.1, s32[16,1024]{1,0:T(8,128)} %spin_hbm.1, bf16[256,512]{1,0:T(8,128)(2,1)} %w_hbm.1, f32[1,256]{1,0:T(1,128)} %bitcast.4, f32[1,256]{1,0:T(1,128)} %bitcast.5, f32[16]{0:T(128)} %e_ref.1, bf16[64,256]{1,0:T(8,128)(2,1)} %bitcast.3, ...), custom_call_target="tpu_custom_call" | custom-call | tf_op jit(solution)/shard_map/pallas_call | solution.py:347
  39.2 0.7 %shard_map.96 = (f32[256,128]{1,0:T(8,128)}, f32[256,128]{1,0:T(8,128)}) custom-call(f32[256,128]{1,0:T(8,128)S(1)} %get-tuple-element.4.a_ref, f32[256,128]{1,0:T(8,128)S(1)} %get-tuple-element.5.b_ref), custom_call_target="tpu_custom_call" | custom-call | tf_op jit(solution)/shard_map/pallas_call | solution.py:392
